TPU v7x, 128 devices: a whole 4x4x4 slice. The times are simulated.
128 devices in a mesh: strip: 8 (over x, z_hi), cuts: 16 (over y, z_lo, core).
Axes of the slice: x: 4, y: 4, z: 4 (z_hi: 2, z_lo: 2; z = z_hi * 2 + z_lo), core: 2. Of those that a mesh axis runs over, the one named last changes fastest.
Arguments:
- start_state: float32 [16, 6, 1024, 512], P('cuts', None, 'strip'), may hold values from -6 to 6
- initial_state: float32 [6, 1024, 512], P(None, 'strip'), may hold values from -6 to 6
- circ_stiff: float32 [1024, 512], P('strip'), may hold values from 0.5 to 2
- axial_stiff: float32 [1024, 512], P('strip'), may hold values from 0.5 to 2
- lumped_mass: float32 [1024, 512], P('strip'), may hold values from 1 to 2
- hoop_stiff: float32 [1024, 512], P('strip'), may hold values from 0.5 to 2
Outputs:
- new_start: float32 [16, 6, 1024, 512], P('cuts', None, 'strip')
- fine_end: float32 [16, 6, 1024, 512], P('cuts', None, 'strip')
All inputs are finite; a program needn't handle non-finite values.
Results may differ from a plain program's by a relative error of at most 0.00002.
Values sent between devices are 32-bit elements; how exact they have to be, the bound alone decides.
A program may use at most 192 MiB of HBM per device.

v0:
```python
import jax
import jax.numpy as jnp
from jax import lax
from jax.sharding import PartitionSpec as P

step_length = 0.35
coupling_fine = 0.25


def shifted(value, axis, steps):
    count = lax.axis_size(axis)
    pairs = [(source, (source + steps) % count) for source in range(count)]
    return lax.ppermute(value, axis, pairs)


def padded_2(cells, sides, width):
    for axis, dim in sides:
        count = lax.axis_size(axis)
        head = lax.slice_in_dim(cells, 0, width, axis=dim)
        tail = lax.slice_in_dim(cells, cells.shape[dim] - width, cells.shape[dim], axis=dim)
        cells = jnp.concatenate(
            [
                lax.ppermute(tail, axis, [(i, (i + 1) % count) for i in range(count)]),
                cells,
                lax.ppermute(head, axis, [((i + 1) % count, i) for i in range(count)]),
            ],
            axis=dim,
        )
    return cells


def from_behind(value, axis, by):
    peers = lax.axis_size(axis)
    pairs = [(i, i + by) for i in range(peers) if 0 <= i + by < peers]
    return lax.ppermute(value, axis, pairs)


def combine_forces(
    displace, above_rows, below_rows, circ_stiff, circ_low, axial_stiff, hoop_stiff, coupling
):
    zero_col = jnp.zeros_like(displace[:, :, :1])
    forward = jnp.concatenate([displace[:, :, 1:], zero_col], axis=2)
    backward = jnp.concatenate([zero_col, displace[:, :, :-1]], axis=2)
    axial_low = jnp.concatenate([jnp.zeros_like(axial_stiff[:, :1]), axial_stiff[:, :-1]], axis=1)
    summed = circ_stiff * (above_rows - displace) + circ_low * (below_rows - displace)
    summed = summed + axial_stiff * (forward - displace) + axial_low * (backward - displace)
    gradient = 0.5 * (above_rows - below_rows)
    first_comp = summed[0] - coupling * gradient[2]
    third_comp = summed[2] + coupling * gradient[0] - hoop_stiff * displace[2]
    return jnp.stack([first_comp, summed[1], third_comp])


def verlet(current, force_fn, masses, increment, repeats):
    displace = current[:3]
    velocity = current[3:]
    acceleration = force_fn(displace) / masses
    for number in range(repeats):
        half_step = velocity + 0.5 * increment * acceleration
        displace = displace + increment * half_step
        acceleration = force_fn(displace) / masses
        velocity = half_step + 0.5 * increment * acceleration
    return jnp.concatenate([displace, velocity], axis=0)


def restrict(field):
    leading = field.shape[:-2]
    rows = field.shape[-2]
    cols = field.shape[-1]
    return field.reshape(leading + (rows // 2, 2, cols // 2, 2)).mean(axis=(-3, -1))


def prolong(field):
    return jnp.repeat(jnp.repeat(field, 2, axis=-2), 2, axis=-1)


def per_device(start_state, initial_state, circ_stiff, axial_stiff, lumped_mass, hoop_stiff):
    current = start_state[0]
    lower_rows = shifted(circ_stiff[-2:], "strip", 1)
    circ_low = jnp.concatenate([lower_rows[1:], circ_stiff[:-1]], axis=0)

    def fine_force(displace):
        padded = padded_2(displace, (("strip", 1),), 1)
        return combine_forces(
            displace,
            padded[:, 2:],
            padded[:, :-2],
            circ_stiff,
            circ_low,
            axial_stiff,
            hoop_stiff,
            coupling_fine,
        )

    fine_end = verlet(current, fine_force, lumped_mass, step_length, 2)
    received = from_behind(fine_end, "cuts", 1)
    position = lax.axis_index("cuts")
    mismatch = jnp.where(position == 0, initial_state - current, received - current)
    coarse_circ = restrict(circ_stiff)
    coarse_low = jnp.concatenate([restrict(lower_rows), coarse_circ[:-1]], axis=0)
    coarse_axial = restrict(axial_stiff)
    coarse_mass = 4.0 * restrict(lumped_mass)
    coarse_hoop = 4.0 * restrict(hoop_stiff)

    def coarse_force(displace):
        padded = padded_2(displace, (("strip", 1),), 1)
        return combine_forces(
            displace,
            padded[:, 2:],
            padded[:, :-2],
            coarse_circ,
            coarse_low,
            coarse_axial,
            coarse_hoop,
            2.0 * coupling_fine,
        )

    residue = restrict(mismatch)
    slices = lax.axis_size("cuts")
    carried = residue
    distance = 1
    while distance < slices:
        moved = from_behind(carried, "cuts", distance)
        for repeat_count in range(distance):
            moved = verlet(moved, coarse_force, coarse_mass, 2.0 * step_length, 1)
        carried = carried + jnp.where(position >= distance, moved, jnp.zeros_like(moved))
        distance = distance * 2
    new_start = current + mismatch + prolong(carried - residue)
    return (new_start[None], fine_end[None])


def solution(mesh):
    placed = (
        P("cuts", None, "strip", None),
        P(None, "strip", None),
        P("strip", None),
        P("strip", None),
        P("strip", None),
        P("strip", None),
    )
    return jax.shard_map(
        per_device,
        mesh=mesh,
        in_specs=placed,
        out_specs=(P("cuts", None, "strip", None), P("cuts", None, "strip", None)),
        check_vma=False,
    )
```

profile of v0, /device:TPU:24, one launch (start us, length us, event | category | flops | bytes accessed | tf_op | source)
XLA Modules:
  0.0 466.5 jit_solution(12202308440864556247)
XLA Ops:
  5.1 6.1 %collective-permute-start = (f32[3,1,512]{2,1,0:T(1,128)S(1)}, f32[3,1,512]{2,1,0:T(1,128)S(1)}, u32[]{:S(2)}, u32[]{:S(2)}) collective-permute-start(f32[3,1,512]{2,1,0:T(1,128)S(1)} %copy.166), channel_id=1, source_target_pairs={{16,0},{32,16},{48,32},{64,48},{80,64},{96,80},{112,96},{0,112},{1... | collective-permute-start | bytes 18440 | tf_op jit(solution)/shard_map/ppermute | solution.py:25
  39.9 4.7 %collective-permute-done.4 = f32[3,1,512]{2,1,0:T(1,128)S(1)} collective-permute-done((f32[3,1,512]{2,1,0:T(1,128)S(1)}, f32[3,1,512]{2,1,0:T(1,128)S(1)}, u32[]{:S(2)}, u32[]{:S(2)}) %collective-permute-start.4) | collective-permute-done | bytes 6176 | tf_op jit(solution)/shard_map/ppermute | solution.py:23
  72.8 18.1 %reshape.86 = f32[64,2,256,2]{3,2,1,0:T(8,128)} reshape(f32[128,512]{1,0:T(8,128)S(1)} %copy-done.7) | data formatting | bytes 524288 | tf_op jit(solution)/shard_map/reshape | solution.py:69
  90.9 18.1 %reshape.87 = f32[64,2,256,2]{3,2,1,0:T(8,128)} reshape(f32[128,512]{1,0:T(8,128)S(1)} %copy-done.9) | data formatting | bytes 524288 | tf_op jit(solution)/shard_map/reshape | solution.py:69
  109.0 18.1 %reshape.88 = f32[64,2,256,2]{3,2,1,0:T(8,128)} reshape(f32[128,512]{1,0:T(8,128)S(1)} %copy-done.17) | data formatting | bytes 524288 | tf_op jit(solution)/shard_map/reshape | solution.py:69
  127.1 18.1 %reshape.89 = f32[64,2,256,2]{3,2,1,0:T(8,128)} reshape(f32[128,512]{1,0:T(8,128)S(1)} %copy-done.18) | data formatting | bytes 524288 | tf_op jit(solution)/shard_map/reshape | solution.py:69
  146.8 8.0 %reduce_sum.64 = f32[64,256]{1,0:T(8,128)S(1)} reduce(f32[64,2,256,2]{3,2,1,0:T(8,128)} %reshape.86, f32[]{:T(128)} %constant.14.clone.1), dimensions={1,3}, to_apply=%region_1.2 | reduce | flops 49152 | bytes 327684 | tf_op jit(solution)/shard_map/reduce_sum | solution.py:69
  154.8 8.6 %reduce_sum.68 = f32[64,256]{1,0:T(8,128)} reduce(f32[64,2,256,2]{3,2,1,0:T(8,128)} %reshape.87, f32[]{:T(128)} %constant.14.clone.1), dimensions={1,3}, to_apply=%region_4.5 | reduce | flops 49152 | bytes 327684 | tf_op jit(solution)/shard_map/reduce_sum | solution.py:69
  163.5 8.0 %reduce_sum.69 = f32[64,256]{1,0:T(8,128)S(1)} reduce(f32[64,2,256,2]{3,2,1,0:T(8,128)} %reshape.88, f32[]{:T(128)} %constant.14.clone.1), dimensions={1,3}, to_apply=%region_5.6 | reduce | flops 49152 | bytes 327684 | tf_op jit(solution)/shard_map/reduce_sum | solution.py:69
  171.5 8.0 %reduce_sum.71 = f32[64,256]{1,0:T(8,128)S(1)} reduce(f32[64,2,256,2]{3,2,1,0:T(8,128)} %reshape.89, f32[]{:T(128)} %constant.14.clone.1), dimensions={1,3}, to_apply=%region_6.7 | reduce | flops 49152 | bytes 327684 | tf_op jit(solution)/shard_map/reduce_sum | solution.py:69
  181.9 15.8 %copy.186 = f32[6,128,512]{0,2,1:T(8,128)} copy(f32[6,128,512]{1,2,0:T(8,128)S(1)} %fusion) | data formatting | bytes 3145728 | tf_op jit(solution)/shard_map/jit(_where)/select_n | solution.py:97
  197.7 32.4 %reduce_sum.63 = f32[6,64,256]{0,2,1:T(8,128)} reduce(f32[6,64,2,256,2]{0,4,3,2,1:T(2,128)} %bitcast.102, f32[]{:T(128)} %constant.14.clone.1), dimensions={2,4}, to_apply=%region_0.1 | reduce | flops 294912 | bytes 1966084 | tf_op jit(solution)/shard_map/reduce_sum | solution.py:69
  230.1 6.3 %copy.187 = f32[6,64,256]{2,1,0:T(8,128)} copy(f32[6,64,256]{0,2,1:T(8,128)} %reduce_sum.63) | data formatting | bytes 786432 | tf_op jit(solution)/shard_map/reduce_sum | solution.py:69
  240.6 6.9 %collective-permute-done.8 = f32[6,64,256]{2,1,0:T(8,128)S(1)} collective-permute-done((f32[6,64,256]{2,1,0:T(8,128)S(1)}, f32[6,64,256]{2,1,0:T(8,128)S(1)}, u32[]{:S(2)}, u32[]{:S(2)}) %collective-permute-start.8) | collective-permute-done | bytes 393248 | tf_op jit(solution)/shard_map/ppermute | solution.py:35
  247.5 5.6 %collective-permute-start.9 = (f32[3,1,256]{2,1,0:T(1,128)S(1)}, f32[3,1,256]{2,1,0:T(1,128)S(1)}, u32[]{:S(2)}, u32[]{:S(2)}) collective-permute-start(f32[3,1,256]{2,1,0:T(1,128)S(1)} %get-tuple-element.108), channel_id=1, source_target_pairs={{16,0},{32,16},{48,32},{64,48},{80,64},{96,80},{112,96},{0,112},{1... | collective-permute-start | bytes 9224 | tf_op jit(solution)/shard_map/ppermute | solution.py:25
  255.0 5.7 %collective-permute-start.11 = (f32[3,1,256]{2,1,0:T(1,128)S(1)}, f32[3,1,256]{2,1,0:T(1,128)S(1)}, u32[]{:S(2)}, u32[]{:S(2)}) collective-permute-start(f32[3,1,256]{2,1,0:T(1,128)S(1)} %get-tuple-element.224), channel_id=1, source_target_pairs={{16,0},{32,16},{48,32},{64,48},{80,64},{96,80},{112,96},{0,112},{1... | collective-permute-start | bytes 9224 | tf_op jit(solution)/shard_map/ppermute | solution.py:25
  262.0 6.0 %collective-permute-done.12 = f32[3,1,256]{2,1,0:T(1,128)S(1)} collective-permute-done((f32[3,1,256]{2,1,0:T(1,128)S(1)}, f32[3,1,256]{2,1,0:T(1,128)S(1)}, u32[]{:S(2)}, u32[]{:S(2)}) %collective-permute-start.12) | collective-permute-done | bytes 3104 | tf_op jit(solution)/shard_map/ppermute | solution.py:23
  271.0 9.0 %collective-permute-done.13 = f32[6,64,256]{2,1,0:T(8,128)} collective-permute-done((f32[6,64,256]{2,1,0:T(8,128)}, f32[6,64,256]{2,1,0:T(8,128)}, u32[]{:S(2)}, u32[]{:S(2)}) %collective-permute-start.13) | collective-permute-done | bytes 393248 | tf_op jit(solution)/shard_map/ppermute | solution.py:35
  280.7 3.5 collective-permute-start.15
  309.9 8.7 %collective-permute-done.20 = f32[6,64,256]{2,1,0:T(8,128)} collective-permute-done((f32[6,64,256]{2,1,0:T(8,128)}, f32[6,64,256]{2,1,0:T(8,128)}, u32[]{:S(2)}, u32[]{:S(2)}) %collective-permute-start.20) | collective-permute-done | bytes 393248 | tf_op jit(solution)/shard_map/ppermute | solution.py:35
  359.0 4.4 collective-permute-done.30
  369.9 7.0 %collective-permute-done.31 = f32[6,64,256]{2,1,0:T(8,128)} collective-permute-done((f32[6,64,256]{2,1,0:T(8,128)}, f32[6,64,256]{2,1,0:T(8,128)}, u32[]{:S(2)}, u32[]{:S(2)}) %collective-permute-start.31) | collective-permute-done | bytes 393248 | tf_op jit(solution)/shard_map/ppermute | solution.py:35
  440.6 4.4 collective-permute-done.47
  445.5 3.6 collective-permute-start.49
  (290 shorter events, 229.3 us)
Async XLA Ops:
  5.1 18.4 %collective-permute-start = (f32[3,1,512]{2,1,0:T(1,128)S(1)}, f32[3,1,512]{2,1,0:T(1,128)S(1)}, u32[]{:S(2)}, u32[]{:S(2)}) collective-permute-start(f32[3,1,512]{2,1,0:T(1,128)S(1)} %copy.166), channel_id=1, source_target_pairs={{16,0},{32,16},{48,32},{64,48},{80,64},{96,80},{112,96},{0,112},{1... | collective-permute-start | bytes 18440 | tf_op jit(solution)/shard_map/ppermute | solution.py:25
  11.5 13.2 %collective-permute-start.2 = (f32[3,1,512]{2,1,0:T(1,128)S(1)}, f32[3,1,512]{2,1,0:T(1,128)S(1)}, u32[]{:S(2)}, u32[]{:S(2)}) collective-permute-start(f32[3,1,512]{2,1,0:T(1,128)S(1)} %copy.169), channel_id=1, source_target_pairs={{0,16},{16,32},{32,48},{48,64},{64,80},{80,96},{96,112},{112,0},{1... | collective-permute-start | bytes 18440 | tf_op jit(solution)/shard_map/ppermute | solution.py:23
  11.6 8.5 %collective-permute-start.1 = (f32[2,512]{1,0:T(2,128)S(1)}, f32[2,512]{1,0:T(2,128)S(1)}, u32[]{:S(2)}, u32[]{:S(2)}) collective-permute-start(f32[2,512]{1,0:T(2,128)S(1)} %slice.1081), channel_id=1, source_target_pairs={{0,16},{16,32},{32,48},{48,64},{64,80},{80,96},{96,112},{112,0},{1... | collective-permute-start | bytes 12296 | tf_op jit(solution)/shard_map/ppermute | solution.py:13
  37.3 7.3 %collective-permute-start.4 = (f32[3,1,512]{2,1,0:T(1,128)S(1)}, f32[3,1,512]{2,1,0:T(1,128)S(1)}, u32[]{:S(2)}, u32[]{:S(2)}) collective-permute-start(f32[3,1,512]{2,1,0:T(1,128)S(1)} %copy.178), channel_id=1, source_target_pairs={{0,16},{16,32},{32,48},{48,64},{64,80},{80,96},{96,112},{112,0},{1... | collective-permute-start | bytes 18440 | tf_op jit(solution)/shard_map/ppermute | solution.py:23
  56.3 7.3 %collective-permute-start.6 = (f32[3,1,512]{2,1,0:T(1,128)S(1)}, f32[3,1,512]{2,1,0:T(1,128)S(1)}, u32[]{:S(2)}, u32[]{:S(2)}) collective-permute-start(f32[3,1,512]{2,1,0:T(1,128)S(1)} %copy.183), channel_id=1, source_target_pairs={{0,16},{16,32},{32,48},{48,64},{64,80},{80,96},{96,112},{112,0},{1... | collective-permute-start | bytes 18440 | tf_op jit(solution)/shard_map/ppermute | solution.py:23
  70.7 109.1 %collective-permute-start.7 = (f32[6,128,512]{1,2,0:T(8,128)}, f32[6,128,512]{1,2,0:T(8,128)}, u32[]{:S(2)}, u32[]{:S(2)}) collective-permute-start(f32[6,128,512]{1,2,0:T(8,128)} %get-tuple-element.37), channel_id=1, source_target_pairs={{0,1},{1,2},{2,3},{3,4},{4,5},{5,6},{6,7},{7,8},{8,9},{9,10},{10,1... | collective-permute-start | bytes 4718600 | tf_op jit(solution)/shard_map/ppermute | solution.py:35
  237.5 10.0 %collective-permute-start.8 = (f32[6,64,256]{2,1,0:T(8,128)S(1)}, f32[6,64,256]{2,1,0:T(8,128)S(1)}, u32[]{:S(2)}, u32[]{:S(2)}) collective-permute-start(f32[6,64,256]{2,1,0:T(8,128)S(1)} %broadcast_multiply_fusion), channel_id=1, source_target_pairs={{0,1},{1,2},{2,3},{3,4},{4,5},{5,6},{6,7},{7,8},{8,9},{9,10},{10,1... | collective-permute-start | bytes 1179656 | tf_op jit(solution)/shard_map/ppermute | solution.py:35
  247.5 7.2 %collective-permute-start.10 = (f32[3,1,256]{2,1,0:T(1,128)S(1)}, f32[3,1,256]{2,1,0:T(1,128)S(1)}, u32[]{:S(2)}, u32[]{:S(2)}) collective-permute-start(f32[3,1,256]{2,1,0:T(1,128)S(1)} %get-tuple-element.109), channel_id=1, source_target_pairs={{0,16},{16,32},{32,48},{48,64},{64,80},{80,96},{96,112},{112,0},{1... | collective-permute-start | bytes 9224 | tf_op jit(solution)/shard_map/ppermute | solution.py:23
  260.7 7.3 %collective-permute-start.12 = (f32[3,1,256]{2,1,0:T(1,128)S(1)}, f32[3,1,256]{2,1,0:T(1,128)S(1)}, u32[]{:S(2)}, u32[]{:S(2)}) collective-permute-start(f32[3,1,256]{2,1,0:T(1,128)S(1)} %get-tuple-element.225), channel_id=1, source_target_pairs={{0,16},{16,32},{32,48},{48,64},{64,80},{80,96},{96,112},{112,0},{1... | collective-permute-start | bytes 9224 | tf_op jit(solution)/shard_map/ppermute | solution.py:23
  269.0 10.9 %collective-permute-start.13 = (f32[6,64,256]{2,1,0:T(8,128)}, f32[6,64,256]{2,1,0:T(8,128)}, u32[]{:S(2)}, u32[]{:S(2)}) collective-permute-start(f32[6,64,256]{2,1,0:T(8,128)} %fusion.8), channel_id=1, source_target_pairs={{0,2},{1,3},{2,4},{3,5},{4,6},{5,7},{6,8},{7,9},{8,10},{9,11},{10,... | collective-permute-start | bytes 1179656 | tf_op jit(solution)/shard_map/ppermute | solution.py:35
  280.7 7.3 %collective-permute-start.15 = (f32[3,1,256]{2,1,0:T(1,128)S(1)}, f32[3,1,256]{2,1,0:T(1,128)S(1)}, u32[]{:S(2)}, u32[]{:S(2)}) collective-permute-start(f32[3,1,256]{2,1,0:T(1,128)S(1)} %get-tuple-element.101), channel_id=1, source_target_pairs={{0,16},{16,32},{32,48},{48,64},{64,80},{80,96},{96,112},{112,0},{1... | collective-permute-start | bytes 9224 | tf_op jit(solution)/shard_map/ppermute | solution.py:23
  290.7 7.2 %collective-permute-start.17 = (f32[3,1,256]{2,1,0:T(1,128)S(1)}, f32[3,1,256]{2,1,0:T(1,128)S(1)}, u32[]{:S(2)}, u32[]{:S(2)}) collective-permute-start(f32[3,1,256]{2,1,0:T(1,128)S(1)} %get-tuple-element.219), channel_id=1, source_target_pairs={{0,16},{16,32},{32,48},{48,64},{64,80},{80,96},{96,112},{112,0},{1... | collective-permute-start | bytes 9224 | tf_op jit(solution)/shard_map/ppermute | solution.py:23
  299.3 7.3 %collective-permute-start.19 = (f32[3,1,256]{2,1,0:T(1,128)S(1)}, f32[3,1,256]{2,1,0:T(1,128)S(1)}, u32[]{:S(2)}, u32[]{:S(2)}) collective-permute-start(f32[3,1,256]{2,1,0:T(1,128)S(1)} %get-tuple-element.214), channel_id=1, source_target_pairs={{0,16},{16,32},{32,48},{48,64},{64,80},{80,96},{96,112},{112,0},{1... | collective-permute-start | bytes 9224 | tf_op jit(solution)/shard_map/ppermute | solution.py:23
  308.6 10.0 %collective-permute-start.20 = (f32[6,64,256]{2,1,0:T(8,128)}, f32[6,64,256]{2,1,0:T(8,128)}, u32[]{:S(2)}, u32[]{:S(2)}) collective-permute-start(f32[6,64,256]{2,1,0:T(8,128)} %fusion.9), channel_id=1, source_target_pairs={{0,4},{1,5},{2,6},{3,7},{4,8},{5,9},{6,10},{7,11},{8,12},{9,13},{1... | collective-permute-start | bytes 1179656 | tf_op jit(solution)/shard_map/ppermute | solution.py:35
  319.4 7.3 %collective-permute-start.22 = (f32[3,1,256]{2,1,0:T(1,128)S(1)}, f32[3,1,256]{2,1,0:T(1,128)S(1)}, u32[]{:S(2)}, u32[]{:S(2)}) collective-permute-start(f32[3,1,256]{2,1,0:T(1,128)S(1)} %get-tuple-element.91), channel_id=1, source_target_pairs={{0,16},{16,32},{32,48},{48,64},{64,80},{80,96},{96,112},{112,0},{1... | collective-permute-start | bytes 9224 | tf_op jit(solution)/shard_map/ppermute | solution.py:23
  329.3 7.2 %collective-permute-start.24 = (f32[3,1,256]{2,1,0:T(1,128)S(1)}, f32[3,1,256]{2,1,0:T(1,128)S(1)}, u32[]{:S(2)}, u32[]{:S(2)}) collective-permute-start(f32[3,1,256]{2,1,0:T(1,128)S(1)} %get-tuple-element.208), channel_id=1, source_target_pairs={{0,16},{16,32},{32,48},{48,64},{64,80},{80,96},{96,112},{112,0},{1... | collective-permute-start | bytes 9224 | tf_op jit(solution)/shard_map/ppermute | solution.py:23
  337.9 7.3 %collective-permute-start.26 = (f32[3,1,256]{2,1,0:T(1,128)S(1)}, f32[3,1,256]{2,1,0:T(1,128)S(1)}, u32[]{:S(2)}, u32[]{:S(2)}) collective-permute-start(f32[3,1,256]{2,1,0:T(1,128)S(1)} %get-tuple-element.203), channel_id=1, source_target_pairs={{0,16},{16,32},{32,48},{48,64},{64,80},{80,96},{96,112},{112,0},{1... | collective-permute-start | bytes 9224 | tf_op jit(solution)/shard_map/ppermute | solution.py:23
  346.3 7.2 %collective-permute-start.28 = (f32[3,1,256]{2,1,0:T(1,128)S(1)}, f32[3,1,256]{2,1,0:T(1,128)S(1)}, u32[]{:S(2)}, u32[]{:S(2)}) collective-permute-start(f32[3,1,256]{2,1,0:T(1,128)S(1)} %get-tuple-element.198), channel_id=1, source_target_pairs={{0,16},{16,32},{32,48},{48,64},{64,80},{80,96},{96,112},{112,0},{1... | collective-permute-start | bytes 9224 | tf_op jit(solution)/shard_map/ppermute | solution.py:23
  356.2 7.2 %collective-permute-start.30 = (f32[3,1,256]{2,1,0:T(1,128)S(1)}, f32[3,1,256]{2,1,0:T(1,128)S(1)}, u32[]{:S(2)}, u32[]{:S(2)}) collective-permute-start(f32[3,1,256]{2,1,0:T(1,128)S(1)} %get-tuple-element.193), channel_id=1, source_target_pairs={{0,16},{16,32},{32,48},{48,64},{64,80},{80,96},{96,112},{112,0},{1... | collective-permute-start | bytes 9224 | tf_op jit(solution)/shard_map/ppermute | solution.py:23
  365.4 11.5 %collective-permute-start.31 = (f32[6,64,256]{2,1,0:T(8,128)}, f32[6,64,256]{2,1,0:T(8,128)}, u32[]{:S(2)}, u32[]{:S(2)}) collective-permute-start(f32[6,64,256]{2,1,0:T(8,128)} %fusion.10), channel_id=1, source_target_pairs={{0,8},{1,9},{2,10},{3,11},{4,12},{5,13},{6,14},{7,15},{16,24},{17,... | collective-permute-start | bytes 1179656 | tf_op jit(solution)/shard_map/ppermute | solution.py:35
  377.7 7.2 %collective-permute-start.33 = (f32[3,1,256]{2,1,0:T(1,128)S(1)}, f32[3,1,256]{2,1,0:T(1,128)S(1)}, u32[]{:S(2)}, u32[]{:S(2)}) collective-permute-start(f32[3,1,256]{2,1,0:T(1,128)S(1)} %get-tuple-element.77), channel_id=1, source_target_pairs={{0,16},{16,32},{32,48},{48,64},{64,80},{80,96},{96,112},{112,0},{1... | collective-permute-start | bytes 9224 | tf_op jit(solution)/shard_map/ppermute | solution.py:23
  387.7 7.2 %collective-permute-start.35 = (f32[3,1,256]{2,1,0:T(1,128)S(1)}, f32[3,1,256]{2,1,0:T(1,128)S(1)}, u32[]{:S(2)}, u32[]{:S(2)}) collective-permute-start(f32[3,1,256]{2,1,0:T(1,128)S(1)} %get-tuple-element.187), channel_id=1, source_target_pairs={{0,16},{16,32},{32,48},{48,64},{64,80},{80,96},{96,112},{112,0},{1... | collective-permute-start | bytes 9224 | tf_op jit(solution)/shard_map/ppermute | solution.py:23
  403.9 7.2 %collective-permute-start.39 = (f32[3,1,256]{2,1,0:T(1,128)S(1)}, f32[3,1,256]{2,1,0:T(1,128)S(1)}, u32[]{:S(2)}, u32[]{:S(2)}) collective-permute-start(f32[3,1,256]{2,1,0:T(1,128)S(1)} %get-tuple-element.177), channel_id=1, source_target_pairs={{0,16},{16,32},{32,48},{48,64},{64,80},{80,96},{96,112},{112,0},{1... | collective-permute-start | bytes 9224 | tf_op jit(solution)/shard_map/ppermute | solution.py:23
  445.5 7.4 %collective-permute-start.49 = (f32[3,1,256]{2,1,0:T(1,128)S(1)}, f32[3,1,256]{2,1,0:T(1,128)S(1)}, u32[]{:S(2)}, u32[]{:S(2)}) collective-permute-start(f32[3,1,256]{2,1,0:T(1,128)S(1)} %get-tuple-element.152), channel_id=1, source_target_pairs={{0,16},{16,32},{32,48},{48,64},{64,80},{80,96},{96,112},{112,0},{1... | collective-permute-start | bytes 9224 | tf_op jit(solution)/shard_map/ppermute | solution.py:23
  (46 other events, 276.1 us)
where the time goes:
time: 475 us; the launch traced here: 467 us
  local copies, waits for them, and re-layouts  154 us (32%)
  waiting for transfers between devices  111 us (23%)
  other arithmetic  101 us (21%)
  starting transfers between devices  97.9 us (21%)
    reshape x4, local copies, waits for them, and re-layouts, restrict(): field.reshape(leading + (rows // 2, 2, cols // 2, 2)).mean(axis=(-3, -1))  72.4 us
    reduce_sum x7, other arithmetic, restrict(): field.reshape(leading + (rows // 2, 2, cols // 2, 2)).mean(axis=(-3, -1))  65.1 us
    ppermute x22, waiting for transfers between devices, padded_2(): lax.ppermute(tail, axis, [(i, (i + 1) % count) for i in range(count)])  58.3 us
    ppermute x22, starting transfers between devices, padded_2(): lax.ppermute(tail, axis, [(i, (i + 1) % count) for i in range(count)])  53.9 us
    ppermute x22, starting transfers between devices, padded_2(): lax.ppermute(head, axis, [((i + 1) % count, i) for i in range(count)])  32 us
    ppermute x5, waiting for transfers between devices, from_behind(): return lax.ppermute(value, axis, pairs)  31.5 us
    ppermute x22, waiting for transfers between devices, padded_2(): lax.ppermute(head, axis, [((i + 1) % count, i) for i in range(count)])  21.4 us
    unnamed x49, local copies, waits for them, and re-layouts  16.5 us
  transfers between devices with their start and end apart: 50, of which 40 were waited for; matrix products, arithmetic and copies ran while one was open for 29% of the time, Pallas kernels for 0%

commit v1 on v0

v1 whole, which is shorter than its diff:
```python
import jax
import jax.numpy as jnp
from jax import lax
from jax.experimental import pallas as pl
from jax.experimental.pallas import tpu as pltpu
from jax.sharding import PartitionSpec as P

MESH = pl.DeviceIdType.MESH
F32 = jnp.float32
BF16 = jnp.bfloat16
fine_t = 0.35
coarse_t = 0.7
fine_k = 0.25
coarse_k = 0.5

FR, FO = 160, 16
CR, CO = 112, 24


def tile(number):
    return pl.multiple_of(number * 8, 8)


def loop(first, last, body):
    def step(number, carry):
        body(tile(number))
        return carry

    lax.fori_loop(first, last, step, 0)


def along(blocks):
    lane = lax.broadcasted_iota(jnp.int32, (8, 128), 1)
    lefts = [pltpu.roll(block, 127, 1) for block in blocks]
    rights = [pltpu.roll(block, 1, 1) for block in blocks]
    forward = []
    backward = []
    for q in range(len(blocks)):
        ahead = lefts[q] if q == len(blocks) - 1 else jnp.where(lane == 127, lefts[q + 1], lefts[q])
        behind = rights[q] if q == 0 else jnp.where(lane == 0, rights[q - 1], rights[q])
        forward.append(ahead)
        backward.append(behind)
    return forward, backward


def derive(raw, out, r, count, increment, coupling):
    lane = lax.broadcasted_iota(jnp.int32, (8, 128), 1)
    axial = [raw[1, q, pl.ds(r, 8), :] for q in range(count)]
    _, before = along(axial)
    for q in range(count):
        scale = (0.5 * increment * increment) / raw[2, q, pl.ds(r, 8), :]
        circ = raw[0, q, pl.ds(r, 8), :] * scale
        below = raw[0, q, pl.ds(r - 1, 8), :] * scale
        ax = axial[q] * scale
        low = before[q] * scale
        if q == 0:
            low = jnp.where(lane == 0, 0.0, low)
        diagonal = circ + below + ax + low
        out[0, q, pl.ds(r, 8), :] = circ
        out[1, q, pl.ds(r, 8), :] = below
        out[2, q, pl.ds(r, 8), :] = jnp.where(lane == 127, 0.0, ax) if q == count - 1 else ax
        out[3, q, pl.ds(r, 8), :] = low
        out[4, q, pl.ds(r, 8), :] = diagonal
        out[5, q, pl.ds(r, 8), :] = diagonal + raw[3, q, pl.ds(r, 8), :] * scale
        out[6, q, pl.ds(r, 8), :] = scale * (0.5 * coupling)


def pull(load, coefs, r, count, kinds):
    result = []
    edges = []
    for i, kind in enumerate(kinds):
        blocks = [load(i, q, 0) for q in range(count)]
        forward, backward = along(blocks)
        values = []
        sides = []
        for q in range(count):
            above = load(i, q, 1)
            below = load(i, q, -1)
            value = coefs[0, q, pl.ds(r, 8), :] * above + coefs[1, q, pl.ds(r, 8), :] * below
            value = value + coefs[2, q, pl.ds(r, 8), :] * forward[q]
            value = value + coefs[3, q, pl.ds(r, 8), :] * backward[q]
            value = value - coefs[5 if kind == 2 else 4, q, pl.ds(r, 8), :] * blocks[q]
            values.append(value)
            sides.append(above - below)
        result.append(values)
        edges.append(sides)
    if 2 in kinds:
        i0, i2 = kinds.index(0), kinds.index(2)
        for q in range(count):
            couple = coefs[6, q, pl.ds(r, 8), :]
            result[i0][q] = result[i0][q] - couple * edges[i2][q]
            result[i2][q] = result[i2][q] + couple * edges[i0][q]
    return result


def split_dot(x, picks):
    first = x.astype(BF16)
    rest = x - first.astype(F32)
    second = rest.astype(BF16)
    third = (rest - second.astype(F32)).astype(BF16)
    total = jnp.dot(third, picks, preferred_element_type=F32) + jnp.dot(second, picks, preferred_element_type=F32)
    return total + jnp.dot(first, picks, preferred_element_type=F32)


def pair_picks(value, down):
    shape = (256, 128) if down else (128, 256)
    long = lax.broadcasted_iota(jnp.int32, shape, 0 if down else 1)
    short = lax.broadcasted_iota(jnp.int32, shape, 1 if down else 0)
    hit = (long == 2 * short) | (long == 2 * short + 1)
    return jnp.where(hit, value, 0.0).astype(BF16)


def restricted(ref, plane, half, rows, picks):
    parts = [ref[plane, 2 * half + q, pl.ds(0, rows, 2), :] + ref[plane, 2 * half + q, pl.ds(1, rows, 2), :] for q in range(2)]
    return split_dot(jnp.concatenate(parts, axis=1), picks)


def barrier_with(devices):
    barrier = pltpu.get_barrier_semaphore()
    for device in devices:
        pl.semaphore_signal(barrier, inc=1, device_id=device, device_id_type=MESH)
    return lambda: pl.semaphore_wait(barrier, len(devices))


def fine_kernel(
    start, initial, circ, axial, mass, hoop, end, step_out, coarse_out,
    data, other, first, coefs, small, small_next, small_coefs, load_sem, send_sem, recv_sem,
):
    me = lax.axis_index("strip")
    strips = lax.axis_size("strip")
    position = lax.axis_index("cuts")
    above = {"strip": lax.rem(me + 1, strips)}
    below = {"strip": lax.rem(me + strips - 1, strips)}
    arrived = barrier_with([below, above])
    loads = []
    for q in range(4):
        lanes = slice(128 * q, 128 * q + 128)
        loads.append(pltpu.make_async_copy(start.at[0, :, :, lanes], data.at[0:6, q, FO:FO + 128], load_sem.at[len(loads)]))
        for n, field in enumerate((circ, axial, mass, hoop)):
            loads.append(pltpu.make_async_copy(field.at[:, lanes], data.at[6 + n, q, FO:FO + 128], load_sem.at[len(loads)]))
    extra = [
        pltpu.make_async_copy(initial.at[:, :, 128 * q:128 * q + 128], first.at[:, q, FO:FO + 128], load_sem.at[len(loads) + q])
        for q in range(4)
    ]
    for copy in loads:
        copy.start()

    @pl.when(position == 0)
    def _():
        for copy in extra:
            copy.start()

    def edges(ref, at):
        return [
            pltpu.make_async_remote_copy(
                ref.at[:, :, FO:FO + 8], ref.at[:, :, FO + 128:FO + 136], send_sem.at[at], recv_sem.at[at],
                device_id=below, device_id_type=MESH,
            ),
            pltpu.make_async_remote_copy(
                ref.at[:, :, FO + 120:FO + 128], ref.at[:, :, FO - 8:FO], send_sem.at[at + 1], recv_sem.at[at + 1],
                device_id=above, device_id_type=MESH,
            ),
        ]

    for copy in loads:
        copy.wait()
    arrived()
    swaps = edges(data, 0)
    for copy in swaps:
        copy.start()
    swaps_first = edges(first, 2)

    @pl.when(position == 0)
    def _():
        for copy in extra:
            copy.wait()
        for copy in swaps_first:
            copy.start()

    for copy in swaps:
        copy.wait()
    raw = data.at[6:10]
    loop(1, 19, lambda r: derive(raw, coefs, r, 4, fine_t, fine_k))
    picks = pair_picks(0.25, True)

    def shrink_start(plane, carry):
        for half in range(2):
            small[plane, half, pl.ds(16, 80), :] = restricted(data, plane, half, 80, picks)
        return carry

    lax.fori_loop(0, 10, shrink_start, 0)

    @pl.when(position == 0)
    def _():
        for copy in swaps_first:
            copy.wait()

        def shrink_first(plane, carry):
            for half in range(2):
                small[plane, half, pl.ds(16, 80), :] = small[plane, half, pl.ds(16, 80), :] - restricted(first, plane, half, 80, picks)
            return carry

        lax.fori_loop(0, 6, shrink_first, 0)

    def fine_step(r, source, target, gain, incoming):
        pulls = pull(lambda i, q, by: source[i, q, pl.ds(r + by, 8), :], coefs, r, 4, (0, 1, 2))
        for i in range(3):
            for q in range(4):
                held = data[3 + i, q, pl.ds(r, 8), :]
                if incoming:
                    held = held * fine_t
                moved = held + pulls[i][q] * gain if gain != 1 else held + pulls[i][q]
                if target is None:
                    data[3 + i, q, pl.ds(r, 8), :] = moved * (1.0 / fine_t)
                else:
                    data[3 + i, q, pl.ds(r, 8), :] = moved
                    target[i, q, pl.ds(r, 8), :] = source[i, q, pl.ds(r, 8), :] + moved

    shift = data.at[0:3]
    loop(1, 19, lambda r: fine_step(r, shift, other, 1, True))
    loop(1, 19, lambda r: fine_step(r, other, shift, 2, False))
    loop(1, 19, lambda r: fine_step(r, shift, None, 1, False))
    stores = [
        pltpu.make_async_copy(data.at[0:6, q, FO:FO + 128], end.at[0, :, :, 128 * q:128 * q + 128], load_sem.at[q])
        for q in range(4)
    ]
    for copy in stores:
        copy.start()

    small_raw = small.at[6:10]

    def shrink_end(plane, carry):
        for half in range(2):
            small_next[plane, half, pl.ds(16, 80), :] = restricted(data, plane, half, 80, picks)
        return carry

    lax.fori_loop(0, 6, shrink_end, 0)

    def coarse_setup(r):
        for q in range(2):
            for n in (2, 3):
                small_raw[n, q, pl.ds(r, 8), :] = 4.0 * small_raw[n, q, pl.ds(r, 8), :]
            for n in range(4):
                coarse_out[n, q, pl.ds(r, 8), :] = small_raw[n, q, pl.ds(r, 8), :]

    loop(2, 12, coarse_setup)
    loop(2, 12, lambda r: derive(small_raw, small_coefs, r, 2, coarse_t, coarse_k))

    def coarse_first(r):
        pulls = pull(lambda i, q, by: small[i, q, pl.ds(r + by, 8), :], small_coefs, r, 2, (0, 1, 2))
        for i in range(3):
            for q in range(2):
                moved = coarse_t * small[3 + i, q, pl.ds(r, 8), :] + pulls[i][q]
                small[3 + i, q, pl.ds(r, 8), :] = moved
                first[i, q, pl.ds(r, 8), :] = small[i, q, pl.ds(r, 8), :] + moved

    def coarse_last(r):
        pulls = pull(lambda i, q, by: first[i, q, pl.ds(r + by, 8), :], small_coefs, r, 2, (0, 1, 2))
        for i in range(3):
            for q in range(2):
                at_w, at_p = ((0, 2), (4, 5), (1, 3))[i]
                moved = small[3 + i, q, pl.ds(r, 8), :] + pulls[i][q]
                step_out[at_w, q, pl.ds(r, 8), :] = small_next[i, q, pl.ds(r, 8), :] - first[i, q, pl.ds(r, 8), :]
                step_out[at_p, q, pl.ds(r, 8), :] = coarse_t * small_next[3 + i, q, pl.ds(r, 8), :] - moved

    loop(2, 12, coarse_first)
    loop(2, 12, coarse_last)
    for copy in stores:
        copy.wait()


def scan_body(system, step_in, coarse_in, out, raw, coefs, got, p_low, p_high, total, came, begin, even, odd, spare_a, spare_b, swapped, send_sem, recv_sem):
    me = lax.axis_index("strip")
    strips = lax.axis_size("strip")
    position = lax.axis_index("cuts")
    y = position // 4
    z = lax.rem(position // 2, 2)
    above = lax.rem(me + 1, strips)
    below = lax.rem(me + strips - 1, strips)
    sibling = {"cuts": position + 1 - 2 * system}
    across = position + 2 - 4 * z
    up = lax.rem(position + 4, 16)
    down = lax.rem(position + 12, 16)
    kinds = ((0, 2), (1,))[system]
    comps = len(kinds)
    planes = 2 * comps
    own = slice(CO, CO + 64)

    def send(source, target, at, device):
        return pltpu.make_async_remote_copy(
            source, target, send_sem.at[at], recv_sem.at[at], device_id=device, device_id_type=MESH
        )

    def body_copy(source, target, at, cut):
        return send(source.at[0:planes, :, own], target.at[0:planes, :, own], at, {"cuts": cut})

    def to_below(source, target, at, cut, rows):
        return send(
            source.at[0:planes, :, CO:CO + rows], target.at[0:planes, :, CO + 64:CO + 64 + rows], at,
            {"strip": below, "cuts": cut},
        )

    def to_above(source, target, at, cut, rows):
        return send(
            source.at[0:planes, :, CO + 64 - rows:CO + 64], target.at[0:planes, :, CO - rows:CO], at,
            {"strip": above, "cuts": cut},
        )

    def three(source, target, at, cut, rows):
        return [to_below(source, target, at + 1, cut, rows), to_above(source, target, at + 2, cut, rows), body_copy(source, target, at, cut)]

    def start(copies):
        for copy in copies:
            copy.start()

    def sent(copies):
        for copy in copies:
            copy.wait_send()

    def landed(copies):
        for copy in copies:
            copy.wait_recv()

    def load(ref, base=0):
        return lambda r: (lambda i, q, by: ref[base + i, q, pl.ds(r + by, 8), :])

    def advance(source, target, gain, first, last, base=0):
        def body(r):
            pulls = pull(load(source, base)(r), coefs, r, 2, kinds)
            for i in range(comps):
                for q in range(2):
                    moved = source[base + comps + i, q, pl.ds(r, 8), :] + (pulls[i][q] * gain if gain != 1 else pulls[i][q])
                    target[comps + i, q, pl.ds(r, 8), :] = moved
                    target[i, q, pl.ds(r, 8), :] = source[base + i, q, pl.ds(r, 8), :] + moved

        loop(first, last, body)

    def settle(source, addend, target, first, last, base=0):
        def body(r):
            pulls = pull(load(source)(r), coefs, r, 2, kinds)
            for i in range(comps):
                for q in range(2):
                    target[comps + i, q, pl.ds(r, 8), :] = (
                        source[comps + i, q, pl.ds(r, 8), :] + pulls[i][q] + addend[base + comps + i, q, pl.ds(r, 8), :]
                    )
                    target[i, q, pl.ds(r, 8), :] = source[i, q, pl.ds(r, 8), :] + addend[base + i, q, pl.ds(r, 8), :]

        loop(first, last, body)

    def propagate(source, steps, addend, target, first, last, base=0, add_base=0, kept=None):
        spares = (spare_a, spare_b)
        for n in range(steps):
            advance(source if n == 0 else spares[(n + 1) % 2], spares[n % 2], 1 if n == 0 else 2, first, last, base if n == 0 else 0)
        settle(spares[(steps + 1) % 2], addend, target, *(kept or (first, last)), add_base)

    mine = 4 * system
    pair = send(step_in.at[4:6], got.at[0:2], 0, sibling) if system == 0 else send(step_in.at[0:4], got.at[0:4], 0, sibling)
    pair_in = send(step_in.at[0:4], got.at[0:4], 0, sibling) if system == 0 else send(step_in.at[4:6], got.at[0:2], 0, sibling)
    start([pair])
    stiff = [
        send(coarse_in.at[:, :, CO:CO + 16], raw.at[:, :, CO + 64:CO + 80], 1, {"strip": below}),
        send(coarse_in.at[:, :, CO + 48:CO + 64], raw.at[:, :, CO - 16:CO], 2, {"strip": above}),
    ]
    start(stiff)

    def copy_in(r):
        for n in range(4):
            for q in range(2):
                raw[n, q, pl.ds(r, 8), :] = coarse_in[n, q, pl.ds(r, 8), :]

    loop(3, 11, copy_in)
    landed(stiff)
    loop(1, 13, lambda r: derive(raw, coefs, r, 2, coarse_t, coarse_k))
    landed([pair_in])
    if system == 0:
        early, early_at, late, late_at = step_in, 0, got, 0
    else:
        early, early_at, late, late_at = got, 0, step_in, 4

    low_near = [to_below(p_low, p_low, 4, position, 8), to_above(p_low, p_low, 5, position, 8)]
    low_far = [to_below(p_low, p_low, 6, across, 8), to_above(p_low, p_low, 7, across, 8), body_copy(p_low, p_low, 3, across)]
    high_far = [body_copy(p_high, p_high, 3, across)]

    @pl.when(z == 0)
    def _():
        propagate(early, 1, late, p_low, 2, 12, early_at, late_at, (3, 11))
        start(low_near + low_far)
        landed(high_far + low_near)

    @pl.when(z == 1)
    def _():
        propagate(early, 1, late, p_high, 2, 12, early_at, late_at, (3, 11))
        start(high_far)
        landed(low_far)

    propagate(p_low, 2, p_high, total, 2, 12)
    next_up = three(total, came, 8, up, 8)
    next_down = three(total, came, 11, down, 16)
    final_up = three(even, begin, 14, up, 8)

    @pl.when(y == 0)
    def _():
        start(next_up + next_down)

        def clear(r):
            for n in range(planes):
                for q in range(2):
                    begin[n, q, pl.ds(r, 8), :] = jnp.zeros((8, 128), F32)

        loop(2, 12, clear)

    @pl.when(y == 1)
    def _():
        start(next_up)
        landed(next_up)
        propagate(came, 4, total, even, 2, 12)
        start(final_up)

        def keep(r):
            for n in range(planes):
                for q in range(2):
                    begin[n, q, pl.ds(r, 8), :] = came[n, q, pl.ds(r, 8), :]

        loop(2, 12, keep)

    @pl.when(y == 2)
    def _():
        landed(next_up)
        propagate(came, 4, total, even, 2, 12)
        start(final_up)
        landed(final_up)

    @pl.when(y == 3)
    def _():
        landed(next_down)
        for n in range(8):
            advance((came, spare_a, spare_b)[0 if n == 0 else 1 + (n + 1) % 2], (spare_a, spare_b)[n % 2], 1 if n == 0 else 2, 1, 13)
        landed(final_up)
        settle(spare_b, begin, odd, 2, 12)

        def keep(r):
            for n in range(planes):
                for q in range(2):
                    begin[n, q, pl.ds(r, 8), :] = odd[n, q, pl.ds(r, 8), :]

        loop(2, 12, keep)

    @pl.when((y == 1) | (y == 2))
    def _():
        sent(final_up)

    @pl.when(z == 0)
    def _():
        def keep(r):
            for n in range(planes):
                for q in range(2):
                    even[n, q, pl.ds(r, 8), :] = begin[n, q, pl.ds(r, 8), :]

        loop(2, 12, keep)

    @pl.when(z == 1)
    def _():
        propagate(begin, 2, p_low, even, 2, 12)

    propagate(even, 1, early, odd, 2, 12, 0, early_at)
    swap = send((odd if system == 0 else even).at[0:planes, :, own], swapped.at[0:planes], 17, sibling)
    swap_in = send(came.at[0:6 - planes, :, own], swapped.at[0:6 - planes], 17, sibling)

    start([swap])
    kept = even if system == 0 else odd
    for n in range(planes):
        out[mine + n] = kept[n, :, CO:CO + 64, :]
    landed([swap_in])
    for n in range(6 - planes):
        out[(4 if system == 0 else 0) + n] = swapped[n]

    sent([pair] + stiff + [swap])

    @pl.when(z == 0)
    def _():
        sent(low_near + low_far)

    @pl.when(z == 1)
    def _():
        sent(high_far)

    @pl.when(y == 0)
    def _():
        sent(next_up + next_down)

    @pl.when(y == 1)
    def _():
        sent(next_up)


def scan_kernel(step_in, coarse_in, out, *scratch):
    me = lax.axis_index("strip")
    strips = lax.axis_size("strip")
    position = lax.axis_index("cuts")
    core = lax.rem(position, 2)
    z = lax.rem(position // 2, 2)
    above = lax.rem(me + 1, strips)
    below = lax.rem(me + strips - 1, strips)
    across = position + 2 - 4 * z
    up = lax.rem(position + 4, 16)
    down = lax.rem(position + 12, 16)
    devices = [{"cuts": position + 1 - 2 * core}, {"strip": above}, {"strip": below}]
    for cut in (across, up, down):
        devices += [{"cuts": cut}, {"strip": above, "cuts": cut}, {"strip": below, "cuts": cut}]
    barrier_with(devices)()
    for system in range(2):
        @pl.when(core == system)
        def _(system=system):
            scan_body(system, step_in, coarse_in, out, *scratch)


def compose_kernel(came, coarse, initial, out, data, load_sem):
    position = lax.axis_index("cuts")

    def copies(source, back):
        pairs = [(source.at[:, :, 128 * q:128 * q + 128], data.at[:, q]) for q in range(4)]
        return [pltpu.make_async_copy(b, a, load_sem.at[q]) if back else pltpu.make_async_copy(a, b, load_sem.at[q]) for q, (a, b) in enumerate(pairs)]

    @pl.when(position == 0)
    def _():
        for copy in copies(initial, False):
            copy.start()
        for copy in copies(initial, False):
            copy.wait()

    @pl.when(position > 0)
    def _():
        for copy in copies(came, False):
            copy.start()
        for copy in copies(came, False):
            copy.wait()
        shrink = pair_picks(0.25, True)
        grow = pair_picks(1.0, False)
        for plane in range(6):
            at, gain = ((0, 1.0), (4, 1.0), (1, 1.0), (2, 1.0 / coarse_t), (5, 1.0 / coarse_t), (3, 1.0 / coarse_t))[plane]
            for half in range(2):
                wanted = coarse[at, half] * gain if plane >= 3 else coarse[at, half]
                spread = split_dot(wanted - restricted(data, plane, half, 64, shrink), grow)
                for q in range(2):
                    for odd in range(2):
                        rows = pl.ds(odd, 64, 2)
                        data[plane, 2 * half + q, rows, :] = data[plane, 2 * half + q, rows, :] + spread[:, 128 * q:128 * q + 128]

    for copy in copies(out.at[0], True):
        copy.start()
    for copy in copies(out.at[0], True):
        copy.wait()


def per_device(start_state, initial_state, circ_stiff, axial_stiff, lumped_mass, hoop_stiff):
    anywhere = pl.BlockSpec(memory_space=pl.ANY)
    inside = pl.BlockSpec(memory_space=pltpu.VMEM)
    field = lambda n, q, rows: pltpu.VMEM((n, q, rows, 128), F32)
    fine_end, step, stiff = pl.pallas_call(
        fine_kernel,
        name="fine",
        out_shape=(
            jax.ShapeDtypeStruct((1, 6, 128, 512), F32),
            jax.ShapeDtypeStruct((6, 2, CR, 128), F32),
            jax.ShapeDtypeStruct((4, 2, CR, 128), F32),
        ),
        in_specs=[anywhere] * 6,
        out_specs=(anywhere, inside, inside),
        scratch_shapes=[
            field(10, 4, FR), field(3, 4, FR), field(6, 4, FR), field(7, 4, FR),
            field(10, 2, CR), field(6, 2, CR), field(7, 2, CR),
            pltpu.SemaphoreType.DMA((24,)), pltpu.SemaphoreType.DMA((4,)), pltpu.SemaphoreType.DMA((4,)),
        ],
        compiler_params=pltpu.CompilerParams(collective_id=0, has_side_effects=True),
        cost_estimate=pl.CostEstimate(flops=30_000_000, bytes_accessed=8_000_000, transcendentals=0),
    )(start_state, initial_state, circ_stiff, axial_stiff, lumped_mass, hoop_stiff)
    cuts = lax.axis_size("cuts")
    came = lax.ppermute(fine_end[0], "cuts", [(i, i + 1) for i in range(cuts - 1)])
    coarse = pl.pallas_call(
        scan_kernel,
        name="scan",
        out_shape=jax.ShapeDtypeStruct((6, 2, 64, 128), F32),
        in_specs=[inside] * 2,
        out_specs=inside,
        scratch_shapes=[field(4, 2, CR), field(7, 2, CR)] + [field(4, 2, CR)] * 10 + [
            field(4, 2, 64),
            pltpu.SemaphoreType.DMA((18,)), pltpu.SemaphoreType.DMA((18,)),
        ],
        compiler_params=pltpu.CompilerParams(collective_id=1, has_side_effects=True),
        cost_estimate=pl.CostEstimate(flops=60_000_000, bytes_accessed=100_000_000, transcendentals=0),
    )(step, stiff)
    new_start = pl.pallas_call(
        compose_kernel,
        name="compose",
        out_shape=jax.ShapeDtypeStruct((1, 6, 128, 512), F32),
        in_specs=[anywhere, inside, anywhere],
        out_specs=anywhere,
        scratch_shapes=[field(6, 4, 128), pltpu.SemaphoreType.DMA((4,))],
        cost_estimate=pl.CostEstimate(flops=1_000_000, bytes_accessed=4_000_000, transcendentals=0),
    )(came, coarse, initial_state)
    return (new_start, fine_end)


def solution(mesh):
    placed = (
        P("cuts", None, "strip", None),
        P(None, "strip", None),
        P("strip", None),
        P("strip", None),
        P("strip", None),
        P("strip", None),
    )
    return jax.shard_map(
        per_device,
        mesh=mesh,
        in_specs=placed,
        out_specs=(P("cuts", None, "strip", None), P("cuts", None, "strip", None)),
        check_vma=False,
    )
```

time: 475 us -> 96.4 us (0.20); the launches traced: 467 us -> 95.7 us
  local copies, waits for them, and re-layouts: 154 us -> 2.29 us
  waiting for transfers between devices: 111 us -> 0.01 us
  other arithmetic: 101 us -> 0 us
  starting transfers between devices: 97.9 us -> 1.92 us
  Pallas kernels: 0 us -> 90.7 us
    ppermute x50 -> x1, waiting for transfers between devices: 111 us -> 0.01 us  [per_device(): lax.ppermute(fine_end[0], 'cuts', [(i, i + 1) for i in range(cuts - 1)])]
    ppermute x50 -> x1, starting transfers between devices: 97.9 us -> 1.92 us  [per_device(): lax.ppermute(fine_end[0], 'cuts', [(i, i + 1) for i in range(cuts - 1)])]
    pallas_call x0 -> x3, Pallas kernels: none -> 90.7 us  [the longest x1 58.4 us: per_device(): pl.pallas_call(scan_kernel, name='scan', out_shape=jax.ShapeDtypeStruct((...]
    reshape x6 -> x0, local copies, waits for them, and re-layouts: 77.2 us -> none  [the longest x4 72.4 us: restrict(): field.reshape(leading + (rows // 2, 2, cols // 2, 2)).mean(axis=(-3, -1))]
    reduce_sum x7 -> x0, other arithmetic: 65.1 us -> none  [restrict(): field.reshape(leading + (rows // 2, 2, cols // 2, 2)).mean(axis=(-3, -1))]
    slice x57 -> x0, local copies, waits for them, and re-layouts: 25.2 us -> none  [the longest x22 8.75 us: combine_forces(): forward = jnp.concatenate([displace[:, :, 1:], zero_col], axis=2)]
    add x47 -> x0, other arithmetic: 23.6 us -> none  [the longest x22 10.3 us: combine_forces(): summed + axial_stiff * (forward - displace)]
    select_n x1 -> x0, local copies, waits for them, and re-layouts: 15.8 us -> none  [per_device(): jnp.where(position == 0, initial_state - current, received - current)]
  transfers between devices with their start and end apart: 50 -> 1, of which waited for: 40 -> 0; matrix products, arithmetic and copies ran while one was open for 29% -> 0% of each run, Pallas kernels for 0% -> 61%
where the time goes in v1:
time: 96.4 us; the launch traced here: 95.7 us
  Pallas kernels  90.7 us (94%)
  local copies, waits for them, and re-layouts  2.29 us (2%)
  starting transfers between devices  1.92 us (2%)
    pallas_call x1, Pallas kernels, per_device(): pl.pallas_call(scan_kernel, name='scan', out_shape=jax.ShapeDtypeStruct((...  58.4 us
    pallas_call x1, Pallas kernels, per_device(): pl.pallas_call(fine_kernel, name='fine', out_shape=(jax.ShapeDtypeStruct(...  27.9 us
    pallas_call x1, Pallas kernels, per_device(): pl.pallas_call(compose_kernel, name='compose', out_shape=jax.ShapeDtypeSt...  4.48 us
    unnamed x5, local copies, waits for them, and re-layouts  2.29 us
  transfers between devices with their start and end apart: 1, of which 0 were waited for; matrix products, arithmetic and copies ran while one was open for 0% of the time, Pallas kernels for 61%

profile of v1, /device:TPU:24, one launch (start us, length us, event | category | flops | bytes accessed | tf_op | source)
XLA Modules:
  0.0 95.7 jit_solution(14561058509300120302)
XLA Ops:
  0.6 27.9 %fine.1 = (f32[1,6,128,512]{3,2,1,0:T(8,128)}, f32[6,2,112,128]{3,2,1,0:T(8,128)}, f32[4,2,112,128]{3,2,1,0:T(8,128)}) custom-call(f32[1,6,128,512]{3,2,1,0:T(8,128)} %start.1, f32[6,128,512]{2,1,0:T(8,128)} %initial.3, f32[128,512]{1,0:T(8,128)} %circ.1, f32[128,512]{1,0:T(8,128)} %axial.1, f32[128,512]{1,0:T(8,128)} %mass.1, f32[128,512]{1,0:T(8,128)} %hoop.1), custom_call_target="tpu_custom_call" | custom-call | flops 30000000 | bytes 8000000 | tf_op jit(solution)/shard_map/fine/pallas_call | solution.py:559
  28.5 1.9 %collective-permute-start = (f32[6,128,512]{2,1,0:T(8,128)}, f32[6,128,512]{2,1,0:T(8,128)S(1)}, u32[]{:S(2)}, u32[]{:S(2)}) collective-permute-start(f32[6,128,512]{2,1,0:T(8,128)} %bitcast.1), channel_id=1, source_target_pairs={{0,1},{1,2},{2,3},{3,4},{4,5},{5,6},{6,7},{7,8},{8,9},{9,10},{10,1... | collective-permute-start | bytes 4718600 | tf_op jit(solution)/shard_map/ppermute | solution.py:578
  30.4 58.4 %scan.1.coarse = f32[6,2,64,128]{3,2,1,0:T(8,128)} custom-call(f32[6,2,112,128]{3,2,1,0:T(8,128)} %get-tuple-element.6.step_in, f32[4,2,112,128]{3,2,1,0:T(8,128)} %get-tuple-element.7.coarse_in), custom_call_target="tpu_custom_call" | custom-call | flops 60000000 | bytes 100000000 | tf_op jit(solution)/shard_map/scan/pallas_call | solution.py:579
  88.8 0.0 copy-start
  88.9 0.0 collective-permute-done.came
  88.9 0.0 copy-start.1
  88.9 1.1 %copy-done.1 = f32[6,128,512]{2,1,0:T(8,128)} copy-done((f32[6,128,512]{2,1,0:T(8,128)}, f32[6,128,512]{2,1,0:T(8,128)S(1)}, u32[]{:S(2)}) %copy-start.1) | copy-done | bytes 1572888
  90.0 4.5 %compose.1 = f32[1,6,128,512]{3,2,1,0:T(8,128)} custom-call(f32[6,128,512]{2,1,0:T(8,128)} %copy-done.1, f32[6,2,64,128]{3,2,1,0:T(8,128)} %scan.1.coarse, f32[6,128,512]{2,1,0:T(8,128)} %initial.3), custom_call_target="tpu_custom_call" | custom-call | flops 1000000 | bytes 4000000 | tf_op jit(solution)/shard_map/compose/pallas_call | solution.py:592
  94.5 0.0 copy-done
  94.5 1.1 %copy.9 = f32[1,6,128,512]{3,2,1,0:T(8,128)} copy(f32[1,6,128,512]{3,2,1,0:T(8,128)S(1)} %copy-done) | data formatting | bytes 3145728
Async XLA Ops:
  28.5 60.4 %collective-permute-start = (f32[6,128,512]{2,1,0:T(8,128)}, f32[6,128,512]{2,1,0:T(8,128)S(1)}, u32[]{:S(2)}, u32[]{:S(2)}) collective-permute-start(f32[6,128,512]{2,1,0:T(8,128)} %bitcast.1), channel_id=1, source_target_pairs={{0,1},{1,2},{2,3},{3,4},{4,5},{5,6},{6,7},{7,8},{8,9},{9,10},{10,1... | collective-permute-start | bytes 4718600 | tf_op jit(solution)/shard_map/ppermute | solution.py:578
  88.8 5.7 %copy-start = (f32[1,6,128,512]{3,2,1,0:T(8,128)S(1)}, f32[1,6,128,512]{3,2,1,0:T(8,128)}, u32[]{:S(2)}) copy-start(f32[1,6,128,512]{3,2,1,0:T(8,128)} %get-tuple-element.11) | copy-start | bytes 4718596
  88.9 1.1 %copy-start.1 = (f32[6,128,512]{2,1,0:T(8,128)}, f32[6,128,512]{2,1,0:T(8,128)S(1)}, u32[]{:S(2)}) copy-start(f32[6,128,512]{2,1,0:T(8,128)S(1)} %collective-permute-done.came) | copy-start | bytes 4718596
